TPU v7x, 512 devices: a whole 4x8x8 slice. The times are simulated.
512 devices in a mesh: tile: 16 (over z, core), depth: 32 (over y, x).
Axes of the slice: x: 4, y: 8, z: 8, core: 2. Of those that a mesh axis runs over, the one named last changes fastest.
Arguments:
- velocity: float32 [3, 512, 96, 2048], P(None, 'depth', None, 'tile'), may hold values from -6 to 6
- metric: float32 [96], replicated, may hold values from 0.5 to 2
- colour_map: bfloat16 [4, 128], replicated, may hold values from 0.049804688 to 1
- counts: int32 [96, 2048], P(None, 'tile'), may hold values from 1 to 512
Outputs:
- rendered: float32 [4, 96, 2048], P(None, 'depth', 'tile')
Inputs may be any that keep to these rules, and one draw needn't show every extreme that they name: `counts`: each pixel's ray passes the cells with z below its count.
All inputs are finite; a program needn't handle non-finite values.
Results may differ from a plain program's by a relative error of at most 0.0003.
Values sent between devices are 32-bit elements; how exact they have to be, the bound alone decides.
A program may use at most 64 MiB of HBM per device.

v0:
```python
import jax
import jax.numpy as jnp
from jax import lax
from jax.sharding import PartitionSpec as P

STENCIL_WEIGHTS = (45.0 / 60.0, -9.0 / 60.0, 1.0 / 60.0)
CRITERION_SCALE = 2.0
VORTEX_SCALE = 4.0
OPTICAL_DEPTH = 4.0


def extended(block, sides, width):
    for axis, dim in sides:
        count = lax.axis_size(axis)
        forward = [(i, i + 1) for i in range(count - 1)]
        forward.append((count - 1, 0))
        backward = [(target, source) for source, target in forward]
        low = lax.ppermute(
            lax.slice_in_dim(block, block.shape[dim] - width, None, axis=dim), axis, forward
        )
        high = lax.ppermute(lax.slice_in_dim(block, 0, width, axis=dim), axis, backward)
        block = jnp.concatenate([low, block, high], axis=dim)
    return block


def prefix(part, axis, combine, identity):
    place = lax.axis_index(axis)
    gathered = lax.all_gather(part, axis)
    state = jnp.zeros_like(part) + jnp.asarray(identity, part.dtype)

    def one(lap, state):
        return combine(state, lax.dynamic_index_in_dim(gathered, lap, 0, False))

    return lax.fori_loop(0, place, one, state)


def interior(padded, keep_dim):
    for dimension in range(3):
        if dimension != keep_dim:
            padded = lax.slice_in_dim(padded, 3, padded.shape[dimension] - 3, axis=dimension)
    return padded


def central(padded, dimension):
    extent = padded.shape[dimension] - 6
    result = None
    for offset, weight in zip((1, 2, 3), STENCIL_WEIGHTS):
        forward = lax.slice_in_dim(padded, 3 + offset, 3 + offset + extent, axis=dimension)
        backward = lax.slice_in_dim(padded, 3 - offset, 3 - offset + extent, axis=dimension)
        result = (
            weight * (forward - backward)
            if result is None
            else result + weight * (forward - backward)
        )
    return result


def gradients(padded, metric_rows):
    tensor = []
    for component in range(3):
        component_field = padded[component]
        stream_slope = central(interior(component_field, 2), 2)
        normal_slope = central(interior(component_field, 1), 1) * metric_rows[None, :, None]
        span_slope = central(interior(component_field, 0), 0)
        tensor.append((stream_slope, normal_slope, span_slope))
    return tensor


def invariants(tensor):
    contraction = jnp.zeros_like(tensor[0][0])
    for source in range(3):
        for target in range(3):
            contraction = contraction + tensor[source][target] * tensor[target][source]
    curl_first = tensor[2][1] - tensor[1][2]
    curl_second = tensor[0][2] - tensor[2][0]
    curl_third = tensor[1][0] - tensor[0][1]
    vortex = jnp.sqrt(curl_first * curl_first + curl_second * curl_second + curl_third * curl_third)
    return (-0.5 * contraction, vortex)


def lookup(colour_map, lowbin, fraction, pieces):
    bin_count = colour_map.shape[1]
    cell_shape = lowbin.shape
    flat_bins = lowbin.reshape(pieces, -1)
    paired_table = jnp.concatenate([colour_map, jnp.roll(colour_map, -1, axis=1)], axis=0)

    def select_bins(bin_block):
        onehot = (
            lax.broadcasted_iota(jnp.int32, (bin_count, bin_block.shape[0]), 0) == bin_block[None]
        ).astype(jnp.bfloat16)
        return jnp.dot(paired_table, onehot, preferred_element_type=jnp.float32)

    picked = lax.map(select_bins, flat_bins)
    picked = jnp.moveaxis(picked, 1, 0).reshape((8,) + cell_shape)
    return (1.0 - fraction) * picked[:4] + fraction * picked[4:]


def render(padded, metric_rows, count_rows, colour_map, first_cell, total_depth, pieces):
    criterion, vortex = invariants(gradients(padded, metric_rows))
    bin_count = colour_map.shape[1]
    bin_level = (bin_count - 1) * 0.5 * (1.0 + jnp.tanh(criterion / CRITERION_SCALE))
    lowbin = jnp.minimum(jnp.floor(bin_level), bin_count - 2).astype(jnp.int32)
    fraction = bin_level - lowbin.astype(jnp.float32)
    values = lookup(colour_map, lowbin, fraction, pieces)
    depth_index = first_cell + lax.broadcasted_iota(jnp.int32, criterion.shape, 0)
    inside = depth_index < count_rows[None]
    extinct = jnp.where(inside, values[0] * (OPTICAL_DEPTH / total_depth), 0.0)
    opacity = -jnp.expm1(-extinct)
    emission = values[1:] * jnp.tanh(vortex / VORTEX_SCALE)[None]
    before = jnp.cumsum(extinct, axis=0) - extinct
    colour = jnp.sum((jnp.exp(-before) * opacity)[None] * emission, axis=1)
    return (colour, jnp.sum(extinct, axis=0))


def add_terms(earlier_sum, later_sum):
    return earlier_sum + later_sum


def per_device(velocity, metric, colour_map, counts):
    slab_depth = velocity.shape[1]
    depth_devices = lax.axis_size("depth")
    total_depth = slab_depth * depth_devices
    padded = extended(velocity, (("tile", 3), ("depth", 1)), 3)
    padded = jnp.pad(padded, ((0, 0), (0, 0), (3, 3), (0, 0)))
    first_cell = lax.axis_index("depth") * slab_depth
    colour, extinct_total = render(
        padded, metric, counts, colour_map, first_cell, total_depth, slab_depth
    )
    before = prefix(extinct_total, "depth", add_terms, jnp.zeros_like(extinct_total))
    partial_terms = jnp.concatenate([jnp.exp(-before)[None] * colour, extinct_total[None]], axis=0)
    summed = lax.psum_scatter(partial_terms, "depth", scatter_dimension=1, tiled=True)
    return jnp.concatenate([summed[:3], -jnp.expm1(-summed[3:])], axis=0)


def solution(mesh):
    in_specs = (P(None, "depth", None, "tile"), P(), P(), P(None, "tile"))
    out_specs = P(None, "depth", "tile")
    return jax.shard_map(
        per_device, mesh=mesh, in_specs=in_specs, out_specs=out_specs, check_vma=False
    )
```

profile of v0, /device:TPU:16, one launch (start us, length us, event | category | flops | bytes accessed | tf_op | source)
XLA Modules:
  0.0 397.3 jit_solution(13361243205472849927)
XLA Ops:
  6.5 4.7 %fusion.92 = (f32[3,16,96,3]{3,2,1,0:T(8,128)S(1)}, f32[3,16,96,3]{3,2,1,0:T(8,128)}) fusion(f32[3,16,96,128]{3,2,1,0:T(8,128)} %param.8), kind=kLoop, calls=%fused_computation.150 | loop fusion | bytes 221184 | tf_op jit(solution)/shard_map/slice | solution.py:19
  11.3 2.4 copy.33
  13.6 8.5 %collective-permute-start.1 = (f32[3,16,96,3]{2,1,3,0:T(8,128)S(1)}, f32[3,16,96,3]{2,1,3,0:T(8,128)S(1)}, u32[]{:S(2)}, u32[]{:S(2)}) collective-permute-start(f32[3,16,96,3]{2,1,3,0:T(8,128)S(1)} %copy.33), channel_id=1, source_target_pairs={{32,0},{64,32},{96,64},{128,96},{160,128},{192,160},{224,192},{256... | collective-permute-start | bytes 165896 | tf_op jit(solution)/shard_map/ppermute | solution.py:21
  22.9 2.3 copy.21
  25.2 2.7 collective-permute-done
  29.1 3.4 collective-permute-start.2
  32.5 4.7 %collective-permute-start.3 = (f32[3,3,96,134]{2,3,1,0:T(8,128)}, f32[3,3,96,134]{2,3,1,0:T(8,128)}, u32[]{:S(2)}, u32[]{:S(2)}) collective-permute-start(f32[3,3,96,134]{2,3,1,0:T(8,128)} %get-tuple-element.86), channel_id=1, source_target_pairs={{1,0},{2,1},{3,2},{4,3},{5,4},{6,5},{7,6},{8,7},{9,8},{10,9},{11,1... | collective-permute-start | bytes 1389320 | tf_op jit(solution)/shard_map/ppermute | solution.py:21
  37.4 8.3 %collective-permute-done.2 = f32[3,3,96,134]{2,3,1,0:T(8,128)} collective-permute-done((f32[3,3,96,134]{2,3,1,0:T(8,128)}, f32[3,3,96,134]{2,3,1,0:T(8,128)}, u32[]{:S(2)}, u32[]{:S(2)}) %collective-permute-start.2) | collective-permute-done | bytes 463136 | tf_op jit(solution)/shard_map/ppermute | solution.py:18
  46.9 5.0 %select_maximum_fusion = f32[3,22,102,134]{2,3,1,0:T(8,128)S(1)} fusion(f32[3,3,96,134]{2,3,1,0:T(8,128)} %collective-permute-done.3, f32[3,3,96,134]{2,3,1,0:T(8,128)} %collective-permute-done.2, f32[3,16,96,3]{2,3,1,0:T(4,128)S(1)} %copy.22, f32[3,16,96,128]{2,3,1,0:T(8,128)S(1)} %copy.21, f32[3,16,96,3]{2,3,1,0:T(4,128)S(1)} %copy.20), kind=kLoop, calls=%fused_computation.8 | loop fusion | flops 10825056 | bytes 7004448 | tf_op jit(solution)/shard_map/concatenate | solution.py:22
  52.8 11.4 %multiply_tanh_fusion = (f32[16,96,128]{1,2,0:T(8,128)}, f32[16,96,128]{1,2,0:T(8,128)S(1)}, f32[16,96,128]{1,2,0:T(8,128)}, f32[16,96,128]{1,2,0:T(8,128)}, f32...) fusion(f32[16,102,134]{1,2,0:T(8,128)S(1)} %get-tuple-element.83, f32[96]{0:T(128)S(1)} %copy-done.3, ...), kind=kLoop, calls=%fused_computation.120 | loop fusion | flops 11599872 | bytes 33816960 | tf_op jit(solution)/shard_map/tanh | solution.py:109
  64.2 7.4 %broadcast_subtract_fusion = (f32[16,96,128]{1,2,0:T(8,128)}, f32[16,96,128]{1,2,0:T(8,128)S(1)}) fusion(f32[22,102,134]{1,2,0:T(8,128)S(1)} %get-tuple-element.81, f32[16,96,128]{1,2,0:T(8,128)} %get-tuple-element.74, f32[16,96,128]{1,2,0:T(8,128)} %get-tuple-element.73, f32[96]{0:T(128)S(1)} %copy-done.3, f32[16,102,134]{1,2,0:T(8,128)S(1)} %get-tuple-element.83, ...), kind=kLoop, calls=%fused_computation.132 | loop fusion | flops 9437184 | bytes 20447616 | tf_op jit(solution)/shard_map/sub | solution.py:95
  71.6 2.4 copy.23
  76.3 29.5 %while.20 = (s32[]{:T(128)}, f32[16,8,12288]{2,1,0:T(8,128)}, s32[16,12288]{1,0:T(8,128)S(1)}, bf16[8,128]{1,0:T(8,128)(2,1)S(1)}, s32[]{:T(128)}) while((s32[]{:T(128)}, f32[16,8,12288]{2,1,0:T(8,128)}, s32[16,12288]{1,0:T(8,128)S(1)}, bf16[8,128]{1,0:T(8,128)(2,1)S(1)}, s32[]{:T(128)}) %tuple.56), condition=%wide.region_1.2_spmd, body=%wide.region_0.1_spmd.sunk | while | flops 26738688 | bytes 542797 | solution.py:93
  82.1 1.8 fusion.97
  89.4 1.8 fusion.97
  93.1 1.8 fusion.97
  105.9 7.5 %fusion.91 = (f32[4,16,12288]{2,0,1:T(4,128)}, f32[4,16,12288]{2,0,1:T(4,128)S(1)}) fusion(f32[8,16,12288]{2,0,1:T(8,128)} %bitcast.49), kind=kLoop, calls=%fused_computation.149 | loop fusion | bytes 12582912 | tf_op jit(solution)/shard_map/slice | solution.py:95
  113.4 5.2 %reshape.24 = f32[4,16,96,128]{3,2,0,1:T(8,128)} reshape(f32[4,16,12288]{2,0,1:T(4,128)} %get-tuple-element.77) | data formatting | bytes 6291456 | tf_op jit(solution)/shard_map/slice | solution.py:95
  118.5 3.3 reshape.25
  121.9 4.1 %fusion.3 = f32[4,16,96,128]{3,2,1,0:T(8,128)S(1)} fusion(f32[4,16,96,128]{3,2,0,1:T(8,128)} %reshape.25, f32[4,16,96,128]{3,2,0,1:T(8,128)} %reshape.24, f32[16,96,128]{2,1,0:T(8,128)} %copy.26, f32[16,96,128]{2,1,0:T(8,128)} %copy.23), kind=kLoop, calls=%fused_computation.14 | loop fusion | flops 2359296 | bytes 11010048 | tf_op jit(solution)/shard_map/add | solution.py:95
  126.8 2.4 copy.28
  131.4 79.3 %all-gather.3.cloned.1.call-done = f32[3072,128]{1,0:T(8,128)} async-done(((f32[96,128]{1,0:T(8,128)}), f32[3072,128]{1,0:T(8,128)}) %all-gather.3.cloned.1.call-update) | async-done | bytes 1572880 | tf_op jit(solution)/shard_map/all_gather | solution.py:28
  210.7 6.7 %while.21 = (s32[]{:T(128)}, f32[96,128]{1,0:T(8,128)S(1)}, s32[]{:T(128)}, f32[32,96,128]{2,1,0:T(8,128)}, s32[]{:T(128)}, /*index=5*/s32[]{:T(128)}, s32[]{:T(128)}) while((s32[]{:T(128)}, f32[96,128]{1,0:T(8,128)S(1)}, s32[]{:T(128)}, f32[32,96,128]{2,1,0:T(8,128)}, s32[]{:T(128)}, /*index=5*/s32[]{:T(128)}, s32[]{:T(128)}) %tuple.57), condition=%wide.region_4.5_spmd, body=%wide.region_3.4_spmd.sunk | while | flops 12293 | bytes 147579 | solution.py:34
  220.2 168.3 %all-reduce.4.cloned.1.call-done = f32[4,96,128]{2,0,1:T(4,128)} async-done(((f32[4,96,128]{2,0,1:T(4,128)}), f32[4,96,128]{2,0,1:T(4,128)}) %all-reduce.4.cloned.1.call-update) | async-done | bytes 196624
  (78 shorter events, 43.9 us)
Async XLA Ops:
  6.5 204.1 %all-gather.3.cloned.1.call-start = ((), (), s32[]{:S(2)}) async-start(), calls=%async_computation | async-start | bytes 1622016 | tf_op jit(solution)/shard_map/all_gather | solution.py:28
  13.6 11.5 %collective-permute-start.1 = (f32[3,16,96,3]{2,1,3,0:T(8,128)S(1)}, f32[3,16,96,3]{2,1,3,0:T(8,128)S(1)}, u32[]{:S(2)}, u32[]{:S(2)}) collective-permute-start(f32[3,16,96,3]{2,1,3,0:T(8,128)S(1)} %copy.33), channel_id=1, source_target_pairs={{32,0},{64,32},{96,64},{128,96},{160,128},{192,160},{224,192},{256... | collective-permute-start | bytes 165896 | tf_op jit(solution)/shard_map/ppermute | solution.py:21
  22.9 5.0 %collective-permute-start = (f32[3,16,96,3]{2,1,3,0:T(8,128)S(1)}, f32[3,16,96,3]{2,1,3,0:T(8,128)S(1)}, u32[]{:S(2)}, u32[]{:S(2)}) collective-permute-start(f32[3,16,96,3]{2,1,3,0:T(8,128)S(1)} %copy.32), channel_id=1, source_target_pairs={{0,32},{32,64},{64,96},{96,128},{128,160},{160,192},{192,224},{224... | collective-permute-start | bytes 165896 | tf_op jit(solution)/shard_map/ppermute | solution.py:18
  25.1 12.1 %copy-start.2 = (bf16[4,128]{1,0:T(4,128)(2,1)S(1)}, bf16[4,128]{1,0:T(4,128)(2,1)}, u32[]{:S(2)}) copy-start(bf16[4,128]{1,0:T(4,128)(2,1)} %param.10) | copy-start | bytes 3076
  29.1 16.6 %collective-permute-start.2 = (f32[3,3,96,134]{2,3,1,0:T(8,128)}, f32[3,3,96,134]{2,3,1,0:T(8,128)}, u32[]{:S(2)}, u32[]{:S(2)}) collective-permute-start(f32[3,3,96,134]{2,3,1,0:T(8,128)} %get-tuple-element.85), channel_id=1, source_target_pairs={{0,1},{1,2},{2,3},{3,4},{4,5},{5,6},{6,7},{7,8},{8,9},{9,10},{10,1... | collective-permute-start | bytes 1389320 | tf_op jit(solution)/shard_map/ppermute | solution.py:18
  32.5 14.4 %collective-permute-start.3 = (f32[3,3,96,134]{2,3,1,0:T(8,128)}, f32[3,3,96,134]{2,3,1,0:T(8,128)}, u32[]{:S(2)}, u32[]{:S(2)}) collective-permute-start(f32[3,3,96,134]{2,3,1,0:T(8,128)} %get-tuple-element.86), channel_id=1, source_target_pairs={{1,0},{2,1},{3,2},{4,3},{5,4},{6,5},{7,6},{8,7},{9,8},{10,9},{11,1... | collective-permute-start | bytes 1389320 | tf_op jit(solution)/shard_map/ppermute | solution.py:21
  52.2 0.7 copy-start.3
  121.9 4.1 %copy-start.1 = (s32[96,128]{1,0:T(8,128)S(1)}, s32[96,128]{1,0:T(8,128)}, u32[]{:S(2)}) copy-start(s32[96,128]{1,0:T(8,128)} %param.11) | copy-start | bytes 147460
  126.8 261.7 %all-reduce.4.cloned.1.call-start = ((), (), s32[]{:S(2)}) async-start(), calls=%async_computation.1 | async-start | bytes 393216
  129.8 87.6 %copy-start = (f32[96,128]{1,0:T(8,128)S(1)}, f32[96,128]{1,0:T(8,128)}, u32[]{:S(2)}) copy-start(f32[96,128]{1,0:T(8,128)} %fusion.73) | copy-start | bytes 147460
Sparse Core Ops, SparseCore 0:
  126.9 83.7 all-gather.2
  218.4 170.0 all-reduce.3
where the time goes:
time: 400 us; the launch traced here: 397 us
  waiting for transfers between devices  260 us (65%)
  other arithmetic  40.2 us (10%)
  local copies, waits for them, and re-layouts  37.4 us (9%)
  matrix products  28.6 us (7%)
  starting transfers between devices  16.7 us (4%)
  between operations  14.3 us (4%)
    unnamed x3, waiting for transfers between devices  168 us
    all_gather x1, waiting for transfers between devices, prefix(): gathered = lax.all_gather(part, axis)  79.3 us
    dot_general x16, matrix products, select_bins(): return jnp.dot(paired_table, onehot, preferred_element_type=jnp.float32)  28.6 us
    slice x3, local copies, waits for them, and re-layouts, lookup(): return (1.0 - fraction) * picked[:4] + fraction * picked[4:]  16 us
    ppermute x2, starting transfers between devices, extended(): lax.ppermute(lax.slice_in_dim(block, 0, width, axis=dim), axis, backward)  13.2 us
    tanh x1, other arithmetic, render(): emission = values[1:] * jnp.tanh(vortex / VORTEX_SCALE)[None]  11.4 us
    ppermute x2, waiting for transfers between devices, extended(): lax.ppermute(lax.slice_in_dim(block, block.shape[dim] - width, None, axis...  10.9 us
  transfers between devices with their start and end apart: 6, of which 5 were waited for; matrix products, arithmetic and copies ran while one was open for 2% of the time, Pallas kernels for 0%

commit v1 on v0

v1 whole, which is shorter than its diff:
```python
import functools

import jax
import jax.numpy as jnp
import numpy as np
from jax import lax
from jax.experimental import pallas as pl
from jax.experimental.pallas import tpu as pltpu
from jax.sharding import PartitionSpec as P

COEF = {1: 45.0, -1: -45.0, 2: -9.0, -2: 9.0, 3: 1.0, -3: -1.0}
VORTEX_SCALE = 4.0
OPTICAL_DEPTH = 4.0
CHUNKS = 4
MESH = pl.DeviceIdType.MESH


def stencil_tables(planes, rows, lanes):
    along_rows = np.zeros((rows, rows), np.float32)
    for row in range(rows):
        for offset, weight in COEF.items():
            if 0 <= row + offset < rows:
                along_rows[row, row + offset] = weight
    along_rows = np.concatenate([along_rows, along_rows], axis=1)
    along_lanes = np.zeros((planes, 2 * lanes, lanes), np.float32)
    for plane in range(planes):
        for lane in range(lanes):
            for offset, weight in COEF.items():
                source = lane + offset
                if source < 0:
                    place = lanes + 8 * plane + source + 3
                elif source >= lanes:
                    place = lanes + 8 * plane + source - lanes + 3
                else:
                    place = source
                along_lanes[plane, place, lane] = weight
    return along_rows.astype(jnp.bfloat16), along_lanes.astype(jnp.bfloat16)


def kernel(
    depth_count,
    tile_count,
    vel_hbm,
    metric_hbm,
    map_hbm,
    counts_hbm,
    rowtab_hbm,
    lanetab_hbm,
    out_ref,
    vel,
    high,
    low,
    dx,
    dy,
    metric_in,
    metric,
    map_in,
    table,
    counts,
    rowtab,
    lanetab,
    edge,
    from_left,
    from_right,
    stage,
    pieces,
    landed,
    load_sem,
    edge_send,
    edge_recv,
    halo_send,
    halo_recv,
    piece_send,
    piece_recv,
    ready_sem,
):
    slab = vel_hbm.shape[1]
    rows, lanes = vel_hbm.shape[2:]
    chunk_rows = rows // CHUNKS
    owners = depth_count // CHUNKS
    me = lax.axis_index("depth")
    tile = lax.axis_index("tile")
    up, down = lax.rem(me + 1, depth_count), lax.rem(me + depth_count - 1, depth_count)
    right, left = lax.rem(tile + 1, tile_count), lax.rem(tile + tile_count - 1, tile_count)

    barrier = pltpu.get_barrier_semaphore()
    for peer in ({"depth": up}, {"depth": down}, {"tile": right}, {"tile": left}):
        pl.semaphore_signal(barrier, inc=1, device_id=peer, device_id_type=MESH)

    loads = [
        pltpu.make_async_copy(vel_hbm.at[c], vel.at[c, pl.ds(3, slab)], load_sem.at[c])
        for c in range(3)
    ]
    for place, (source, target) in enumerate(
        (
            (rowtab_hbm, rowtab),
            (metric_hbm, metric_in),
            (lanetab_hbm, lanetab),
            (map_hbm, map_in),
            (counts_hbm, counts),
        )
    ):
        loads.append(pltpu.make_async_copy(source, target, load_sem.at[3 + place]))
    for load in loads:
        load.start()

    def chunk_of(device, step):
        own = device // owners
        return lax.rem(own + jnp.where(step == 0, 2, jnp.where(step == 1, 1, jnp.where(step == 2, 3, 0))), CHUNKS)

    def chunk_at(device, step):
        return pl.ds(pl.multiple_of(chunk_of(device, step) * chunk_rows, 8), chunk_rows)

    def halo_copy(step, upward):
        target = up if upward else down
        window = chunk_at(target, step)
        first, place = (slab - 3, 0) if upward else (0, slab + 3)
        return pltpu.make_async_remote_copy(
            src_ref=vel_hbm.at[:, pl.ds(first, 3), window, :],
            dst_ref=vel.at[:, pl.ds(place, 3), window, :],
            send_sem=halo_send.at[int(upward), step],
            recv_sem=halo_recv.at[int(upward), step],
            device_id={"depth": target},
            device_id_type=MESH,
        )

    def halo_arrival(step, upward):
        window = chunk_at(me, step)
        place = 0 if upward else slab + 3
        part = vel.at[:, pl.ds(place, 3), window, :]
        return pltpu.make_async_copy(part, part, halo_recv.at[int(upward), step])

    def greet(level):
        for peer in (
            lax.rem(me + 2**level, depth_count),
            lax.rem(me + depth_count - 2**level, depth_count),
        ):
            pl.semaphore_signal(
                ready_sem.at[level], inc=1, device_id={"depth": peer}, device_id_type=MESH
            )

    pl.semaphore_wait(barrier, 4)
    for step in range(CHUNKS):
        for upward in (True, False):
            halo_copy(step, upward).start()
    greet(0)

    for load in loads[:3]:
        load.wait()

    lane = lax.broadcasted_iota(jnp.int32, (8, lanes), 1)

    def pack(place, carry):
        component = place // (rows // 8)
        window = pl.ds(pl.multiple_of(lax.rem(place, rows // 8) * 8, 8), 8)
        packed = jnp.zeros((8, lanes), jnp.float32)
        for plane in range(slab):
            turned = pltpu.roll(vel[component, 3 + plane, window, :], (8 * plane + 3) % lanes, 1)
            packed = jnp.where(lane // 8 == plane, turned, packed)
        edge[component, window, :] = packed
        return carry

    lax.fori_loop(0, 3 * rows // 8, pack, 0)

    edge_copies = [
        pltpu.make_async_remote_copy(
            src_ref=edge,
            dst_ref=target,
            send_sem=edge_send.at[place],
            recv_sem=edge_recv.at[place],
            device_id={"tile": peer},
            device_id_type=MESH,
        )
        for place, (target, peer) in enumerate(((from_left, right), (from_right, left)))
    ]
    for copy in edge_copies:
        copy.start()

    pl.semaphore_wait(ready_sem.at[0], 2)
    greet(1)

    for load in loads[3:]:
        load.wait()
    diagonal = lax.broadcasted_iota(jnp.int32, (rows, rows), 0) == lax.broadcasted_iota(
        jnp.int32, (rows, rows), 1
    )
    column = jnp.sum(
        jnp.where(diagonal, jnp.broadcast_to(metric_in[...], (rows, rows)), 0.0),
        axis=1,
        keepdims=True,
    )
    metric[...] = jnp.broadcast_to(column, (rows, lanes))
    entries = map_in[...].astype(jnp.float32)
    steps = pltpu.roll(entries, lanes - 1, 1) - entries
    for channel in range(4):
        table[channel] = jnp.broadcast_to(entries[channel : channel + 1], (8, lanes))
        table[4 + channel] = jnp.broadcast_to(steps[channel : channel + 1], (8, lanes))

    def row_slopes(place, carry):
        component, pair = place // (slab // 2), lax.rem(place, slab // 2)
        first = 2 * pair
        both = jnp.concatenate([vel[component, 3 + first], vel[component, 4 + first]], axis=1)
        upper = both.astype(jnp.bfloat16)
        lower = (both - upper.astype(jnp.float32)).astype(jnp.bfloat16)
        slopes = jnp.dot(
            rowtab[...],
            jnp.concatenate([upper, lower], axis=0),
            preferred_element_type=jnp.float32,
        )
        for half in range(2):
            part = slice(half * lanes, (half + 1) * lanes)
            high[component, first + half] = upper[:, part]
            low[component, first + half] = lower[:, part]
            dy[component, first + half] = slopes[:, part] * metric[...]
        return carry

    lax.fori_loop(0, 3 * slab // 2, row_slopes, 0)

    pl.semaphore_wait(ready_sem.at[1], 2)
    greet(2)
    for copy in edge_copies:
        copy.wait()

    wide_lane = lax.broadcasted_iota(jnp.int32, (3, rows, lanes), 2)
    halo = jnp.where(lax.rem(wide_lane, 8) < 3, from_left[...], from_right[...])
    halo_high = halo.astype(jnp.bfloat16)
    edge_high = halo_high.reshape(3 * rows, lanes)
    edge_low = (halo - halo_high.astype(jnp.float32)).astype(jnp.bfloat16).reshape(3 * rows, lanes)

    def lane_slopes(plane, carry):
        weights = lanetab[plane]
        upper = jnp.concatenate([high[:, plane].reshape(3 * rows, lanes), edge_high], axis=1)
        lower = jnp.concatenate([low[:, plane].reshape(3 * rows, lanes), edge_low], axis=1)
        slopes = jnp.dot(upper, weights, preferred_element_type=jnp.float32) + jnp.dot(
            lower, weights, preferred_element_type=jnp.float32
        )
        dx[:, plane] = slopes.reshape(3, rows, lanes)
        return carry

    lax.fori_loop(0, slab, lane_slopes, 0)

    pl.semaphore_wait(ready_sem.at[2], 2)
    greet(3)

    first_cell = me * slab

    def render(window):
        left_over = counts[window, :] - first_cell
        clear = jnp.ones((8, lanes), jnp.float32)
        total = jnp.zeros((8, lanes), jnp.float32)
        colour = [jnp.zeros((8, lanes), jnp.float32) for _ in range(3)]
        for plane in range(slab):
            slope = []
            for component in range(3):
                field = [vel[component, plane + k, window, :] for k in (0, 1, 2, 4, 5, 6)]
                along = (
                    45.0 * (field[3] - field[2]) - 9.0 * (field[4] - field[1]) + (field[5] - field[0])
                )
                slope.append(
                    (dx[component, plane, window, :], dy[component, plane, window, :], along)
                )
            contraction = (
                slope[0][0] * slope[0][0]
                + slope[1][1] * slope[1][1]
                + slope[2][2] * slope[2][2]
                + 2.0
                * (
                    slope[0][1] * slope[1][0]
                    + slope[0][2] * slope[2][0]
                    + slope[1][2] * slope[2][1]
                )
            )
            curl = (
                slope[2][1] - slope[1][2],
                slope[0][2] - slope[2][0],
                slope[1][0] - slope[0][1],
            )
            square = curl[0] * curl[0] + curl[1] * curl[1] + curl[2] * curl[2]
            swirl = jnp.tanh(
                square * lax.rsqrt(jnp.maximum(square, 1e-30)) * (1.0 / (60.0 * VORTEX_SCALE))
            )
            scale = 0.5 * (lanes - 1)
            level = scale + scale * jnp.tanh(contraction * (-1.0 / (4.0 * 3600.0)))
            bins = jnp.minimum(level.astype(jnp.int32), lanes - 2)
            fraction = level - bins.astype(jnp.float32)
            values = [
                jnp.take_along_axis(table[channel], bins, axis=1, mode="promise_in_bounds")
                + fraction
                * jnp.take_along_axis(table[4 + channel], bins, axis=1, mode="promise_in_bounds")
                for channel in range(4)
            ]
            extinct = jnp.where(
                left_over > plane, values[0] * (OPTICAL_DEPTH / (slab * depth_count)), 0.0
            )
            opacity = extinct * (
                1.0 - extinct * (0.5 - extinct * (1.0 / 6.0 - extinct * (1.0 / 24.0)))
            )
            weight = clear * opacity
            clear = clear - weight
            total = total + extinct
            weight = weight * swirl
            colour = [colour[k] + weight * values[1 + k] for k in range(3)]
        return colour + [total]

    def piece_copy(owner):
        return pltpu.make_async_remote_copy(
            src_ref=pieces.at[owner],
            dst_ref=landed.at[me],
            send_sem=piece_send.at[owner],
            recv_sem=piece_recv.at[me],
            device_id={"depth": owner},
            device_id_type=MESH,
        )

    def render_chunk(step, carry):
        for upward in (True, False):
            halo_arrival(step, upward).wait()
        chunk = chunk_of(me, step)

        def render_rows(part, carry):
            window = pl.ds(pl.multiple_of(chunk * chunk_rows + part * 8, 8), 8)
            for channel, image in enumerate(render(window)):
                stage[channel, pl.ds(pl.multiple_of(part * 8, 8), 8), :] = image
            return carry

        lax.fori_loop(0, chunk_rows // 8, render_rows, 0)
        for row in range(3):
            for channel in range(4):
                spread = stage.at[channel][pl.ds(row, owners, stride=3), :]
                for owner in range(owners):
                    pieces[chunk * owners + owner, pl.ds(4 * row + channel, 1), :] = spread[
                        owner : owner + 1
                    ]

        @pl.when(step == 0)
        def _():
            pl.semaphore_wait(ready_sem.at[3], 2)

        def send(place, carry):
            owner = chunk * owners + place

            @pl.when(owner != me)
            def _():
                piece_copy(owner).start()

            return carry

        lax.fori_loop(0, owners, send, 0)
        return carry

    lax.fori_loop(0, CHUNKS, render_chunk, 0)
    landed[me] = pieces[me]

    def receive(place, carry):
        @pl.when(place != me)
        def _():
            pltpu.make_async_copy(landed.at[place], landed.at[place], piece_recv.at[place]).wait()

        return carry

    lax.fori_loop(0, depth_count, receive, 0)

    before = jnp.zeros((3, lanes), jnp.float32)
    colour = [jnp.zeros((3, lanes), jnp.float32) for _ in range(3)]
    for device in range(depth_count):
        part = [landed.at[device][pl.ds(channel, 3, stride=4), :] for channel in range(4)]
        clear = jnp.exp(-before)
        colour = [colour[k] + clear * part[k] for k in range(3)]
        before = before + part[3]
    for channel, image in enumerate(colour + [before]):
        out_ref[channel] = image

    def sent(place, carry):
        @pl.when(place != me)
        def _():
            piece_copy(place).wait_send()

        return carry

    lax.fori_loop(0, depth_count, sent, 0)
    for step in range(CHUNKS):
        for upward in (True, False):
            halo_copy(step, upward).wait_send()


def per_device(depth_count, tile_count, velocity, metric, colour_map, counts):
    slab, rows, lanes = velocity.shape[1:]
    row_table, lane_table = stencil_tables(slab, rows, lanes)
    f32, bf16 = jnp.float32, jnp.bfloat16
    operands = (
        velocity,
        metric.reshape(1, rows),
        colour_map,
        counts,
        jnp.asarray(row_table),
        jnp.asarray(lane_table),
    )
    result = pl.pallas_call(
        functools.partial(kernel, depth_count, tile_count),
        out_shape=jax.ShapeDtypeStruct((4, rows // depth_count, lanes), f32),
        in_specs=[pl.BlockSpec(memory_space=pl.ANY)] * len(operands),
        out_specs=pl.BlockSpec(memory_space=pltpu.VMEM),
        scratch_shapes=[
            pltpu.VMEM((3, slab + 6, rows, lanes), f32),
            pltpu.VMEM((3, slab, rows, lanes), bf16),
            pltpu.VMEM((3, slab, rows, lanes), bf16),
            pltpu.VMEM((3, slab, rows, lanes), f32),
            pltpu.VMEM((3, slab, rows, lanes), f32),
            pltpu.VMEM((1, rows), f32),
            pltpu.VMEM((rows, lanes), f32),
            pltpu.VMEM(colour_map.shape, bf16),
            pltpu.VMEM((8, 8, lanes), f32),
            pltpu.VMEM((rows, lanes), jnp.int32),
            pltpu.VMEM(row_table.shape, bf16),
            pltpu.VMEM(lane_table.shape, bf16),
            pltpu.VMEM((3, rows, lanes), f32),
            pltpu.VMEM((3, rows, lanes), f32),
            pltpu.VMEM((3, rows, lanes), f32),
            pltpu.VMEM((4, rows // CHUNKS, lanes), f32),
            pltpu.VMEM((depth_count, 16, lanes), f32),
            pltpu.VMEM((depth_count, 16, lanes), f32),
            pltpu.SemaphoreType.DMA((8,)),
            pltpu.SemaphoreType.DMA((2,)),
            pltpu.SemaphoreType.DMA((2,)),
            pltpu.SemaphoreType.DMA((2, CHUNKS)),
            pltpu.SemaphoreType.DMA((2, CHUNKS)),
            pltpu.SemaphoreType.DMA((depth_count,)),
            pltpu.SemaphoreType.DMA((depth_count,)),
            pltpu.SemaphoreType.REGULAR((4,)),
        ],
        compiler_params=pltpu.CompilerParams(
            collective_id=0, has_side_effects=True, vmem_limit_bytes=60 * 1024 * 1024
        ),
    )(*operands)
    channel = lax.broadcasted_iota(jnp.int32, result.shape, 0)
    return jnp.where(channel == 3, -jnp.expm1(-result), result)


def solution(mesh):
    in_specs = (P(None, "depth", None, "tile"), P(), P(), P(None, "tile"))
    out_specs = P(None, "depth", "tile")
    return jax.shard_map(
        functools.partial(per_device, mesh.shape["depth"], mesh.shape["tile"]),
        mesh=mesh,
        in_specs=in_specs,
        out_specs=out_specs,
        check_vma=False,
    )
```

time: 400 us -> 36.9 us (0.09)
  the two profiles are of different devices: /device:TPU:16 before, /device:TPU:6 now
where the time goes in v1:
time: 36.9 us; the launch traced here: 36.8 us
  Pallas kernels  35.4 us (96%)
  other arithmetic  0.78 us (2%)
  local copies, waits for them, and re-layouts  0.6 us (2%)
    pallas_call x1, Pallas kernels, per_device(): pl.pallas_call(functools.partial(kernel, depth_count, tile_count), out_sh...  35.4 us
    select_n x1, other arithmetic, per_device(): return jnp.where(channel == 3, -jnp.expm1(-result), result)  0.77 us

profile of v1, /device:TPU:6, one launch (start us, length us, event | category | flops | bytes accessed | tf_op | source)
XLA Modules:
  0.0 36.8 jit_solution(6664815283455718651)
XLA Ops:
  0.0 35.4 %shard_map.64 = f32[4,3,128]{2,1,0:T(4,128)} custom-call(f32[3,16,96,128]{3,2,1,0:T(8,128)} %vel_hbm.1, f32[1,96]{1,0:T(1,128)} %bitcast.1, bf16[4,128]{1,0:T(4,128)(2,1)} %map_hbm.1, s32[96,128]{1,0:T(8,128)} %counts_hbm.1, bf16[96,192]{1,0:T(8,128)(2,1)} %constant.6.clone.rowtab_hbm, bf16[16,256,128]{2,1,0:T(8,128)(2,1)} %constant.7.clone.lanetab_hbm), custom_call_target="tpu_custom_call" | custom-call | tf_op jit(solution)/shard_map/pallas_call | solution.py:398
  35.4 0.8 %negate_select_fusion = f32[4,3,128]{2,1,0:T(4,128)S(1)} fusion(f32[4,3,128]{2,1,0:T(4,128)} %shard_map.64, pred[4]{0:T(512)(128)(4,1)S(1)} %iota_compare_fusion), kind=kLoop, calls=%fused_computation | loop fusion | flops 4608 | bytes 12292 | tf_op jit(solution)/shard_map/jit(_where)/select_n | solution.py:436
  36.2 0.6 %copy.7 = f32[4,3,128]{2,0,1:T(4,128)} copy(f32[4,3,128]{2,1,0:T(4,128)S(1)} %negate_select_fusion) | data formatting | bytes 12288 | tf_op jit(solution)/shard_map/jit(_where)/select_n | solution.py:436
  (1 shorter events, 0.0 us)

commit v2 on v1

v2 whole, which is shorter than its diff:
```python
import functools

import jax
import jax.numpy as jnp
import numpy as np
from jax import lax
from jax.experimental import pallas as pl
from jax.experimental.pallas import tpu as pltpu
from jax.sharding import PartitionSpec as P

COEF = {1: 45.0, -1: -45.0, 2: -9.0, -2: 9.0, 3: 1.0, -3: -1.0}
VORTEX_SCALE = 4.0
OPTICAL_DEPTH = 4.0
CHUNKS = 4
MESH = pl.DeviceIdType.MESH
ALONG_LANES = lax.GatherDimensionNumbers(
    offset_dims=(),
    collapsed_slice_dims=(1,),
    start_index_map=(1,),
    operand_batching_dims=(0,),
    start_indices_batching_dims=(0,),
)


def stencil_tables(planes, rows, lanes):
    along_rows = np.zeros((rows, rows), np.float32)
    for row in range(rows):
        for offset, weight in COEF.items():
            if 0 <= row + offset < rows:
                along_rows[row, row + offset] = weight
    along_rows = np.concatenate([along_rows, along_rows], axis=1)
    along_lanes = np.zeros((lanes, lanes), np.float32)
    from_halo = np.zeros((planes // 2, lanes, 2 * lanes), np.float32)
    for lane in range(lanes):
        for offset, weight in COEF.items():
            source = lane + offset
            if 0 <= source < lanes:
                along_lanes[source, lane] = weight
                continue
            slot = source + 3 if source < 0 else source - lanes + 3
            for plane in range(planes):
                from_halo[plane // 2, 8 * plane + slot, plane % 2 * lanes + lane] = weight
    return tuple(table.astype(jnp.bfloat16) for table in (along_rows, along_lanes, from_halo))


def lookup(table, bins):
    return lax.gather(
        table,
        bins[..., None],
        ALONG_LANES,
        slice_sizes=(1, 1),
        mode=lax.GatherScatterMode.PROMISE_IN_BOUNDS,
    )


def kernel(
    depth_count,
    tile_count,
    vel_hbm,
    metric_hbm,
    map_hbm,
    counts_hbm,
    rowtab_hbm,
    lanetab_hbm,
    halotab_hbm,
    out_ref,
    vel,
    high,
    low,
    dx,
    dy,
    rest,
    spin,
    span,
    metric_in,
    metric,
    map_in,
    table,
    counts,
    rowtab,
    lanetab,
    halotab,
    edge,
    from_left,
    from_right,
    edge_parts,
    stage,
    pieces,
    landed,
    load_sem,
    edge_send,
    edge_recv,
    halo_send,
    halo_recv,
    piece_send,
    piece_recv,
    ready_sem,
    tile_sem,
):
    slab = vel_hbm.shape[1]
    rows, lanes = vel_hbm.shape[2:]
    chunk_rows = rows // CHUNKS
    owners = depth_count // CHUNKS
    me = lax.axis_index("depth")
    tile = lax.axis_index("tile")
    odd = lax.rem(tile, 2)
    up, down = lax.rem(me + 1, depth_count), lax.rem(me + depth_count - 1, depth_count)
    right, left = lax.rem(tile + 1, tile_count), lax.rem(tile + tile_count - 1, tile_count)

    barrier = pltpu.get_barrier_semaphore()
    for peer in (up, down):
        pl.semaphore_signal(barrier, inc=1, device_id={"depth": peer}, device_id_type=MESH)

    @pl.when(odd == 0)
    def _():
        for peer in (right, left):
            pl.semaphore_signal(barrier, inc=1, device_id={"tile": peer}, device_id_type=MESH)

    loads = [
        pltpu.make_async_copy(vel_hbm.at[c], vel.at[c, pl.ds(3, slab)], load_sem.at[c])
        for c in range(3)
    ]
    for place, (source, target) in enumerate(
        (
            (rowtab_hbm, rowtab),
            (metric_hbm, metric_in),
            (lanetab_hbm, lanetab),
            (map_hbm, map_in),
            (counts_hbm, counts),
            (halotab_hbm, halotab),
        )
    ):
        loads.append(pltpu.make_async_copy(source, target, load_sem.at[3 + place]))
    for load in loads:
        load.start()

    def chunk_of(device, step):
        own = device // owners
        return lax.rem(
            own + jnp.where(step == 0, 2, jnp.where(step == 1, 1, jnp.where(step == 2, 3, 0))),
            CHUNKS,
        )

    def chunk_at(device, step):
        return pl.ds(pl.multiple_of(chunk_of(device, step) * chunk_rows, 8), chunk_rows)

    def halo_copy(step, upward):
        target = up if upward else down
        window = chunk_at(target, step)
        first, place = (slab - 3, 0) if upward else (0, slab + 3)
        return pltpu.make_async_remote_copy(
            src_ref=vel_hbm.at[:, pl.ds(first, 3), window, :],
            dst_ref=vel.at[:, pl.ds(place, 3), window, :],
            send_sem=halo_send.at[int(upward), step],
            recv_sem=halo_recv.at[int(upward), step],
            device_id={"depth": target},
            device_id_type=MESH,
        )

    def halo_arrival(step, upward):
        window = chunk_at(me, step)
        place = 0 if upward else slab + 3
        part = vel.at[:, pl.ds(place, 3), window, :]
        return pltpu.make_async_copy(part, part, halo_recv.at[int(upward), step])

    def edge_copy(component, rightward):
        target = (from_left if rightward else from_right).at[component]
        return pltpu.make_async_remote_copy(
            src_ref=edge.at[component],
            dst_ref=target,
            send_sem=edge_send.at[int(rightward), component],
            recv_sem=edge_recv.at[int(rightward), component],
            device_id={"tile": right if rightward else left},
            device_id_type=MESH,
        )

    def greet(level):
        for peer in (
            lax.rem(me + 2**level, depth_count),
            lax.rem(me + depth_count - 2**level, depth_count),
        ):
            pl.semaphore_signal(
                ready_sem.at[level], inc=1, device_id={"depth": peer}, device_id_type=MESH
            )

    pl.semaphore_wait(barrier, 2 + 2 * odd)
    for step in range(CHUNKS):
        for upward in (True, False):
            halo_copy(step, upward).start()
    greet(0)

    @pl.when(odd == 1)
    def _():
        for peer in (right, left):
            pl.semaphore_signal(tile_sem, inc=1, device_id={"tile": peer}, device_id_type=MESH)

    for component in range(3):
        loads[component].wait()

        def pack(part, carry):
            window = pl.ds(pl.multiple_of(part * 24, 8), 24)
            lane = lax.broadcasted_iota(jnp.int32, (24, lanes), 1)
            packed = jnp.zeros((24, lanes), jnp.float32)
            for plane in range(slab):
                turned = pltpu.roll(
                    vel[component, 3 + plane, window, :], (8 * plane + 3) % lanes, 1
                )
                packed = jnp.where(lane // 8 == plane, turned, packed)
            edge[component, window, :] = packed
            return carry

        lax.fori_loop(0, rows // 24, pack, 0)

        @pl.when(odd == 1)
        def _():
            for rightward in (True, False):
                edge_copy(component, rightward).start()

    pl.semaphore_wait(ready_sem.at[0], 2)
    greet(1)

    for load in loads[3:]:
        load.wait()
    diagonal = lax.broadcasted_iota(jnp.int32, (rows, rows), 0) == lax.broadcasted_iota(
        jnp.int32, (rows, rows), 1
    )
    column = jnp.sum(
        jnp.where(diagonal, jnp.broadcast_to(metric_in[...], (rows, rows)), 0.0),
        axis=1,
        keepdims=True,
    )
    metric[...] = jnp.broadcast_to(column, (rows, lanes))
    entries = map_in[...].astype(jnp.float32)
    steps = pltpu.roll(entries, lanes - 1, 1) - entries
    for channel in range(4):
        table[channel] = jnp.broadcast_to(entries[channel : channel + 1], (8, lanes))
        table[4 + channel] = jnp.broadcast_to(steps[channel : channel + 1], (8, lanes))

    def row_slopes(trip, carry):
        component = trip // 2
        for part in range(4):
            first = 2 * (4 * lax.rem(trip, 2) + part)
            both = jnp.concatenate([vel[component, 3 + first], vel[component, 4 + first]], axis=1)
            upper = both.astype(jnp.bfloat16)
            lower = (both - upper.astype(jnp.float32)).astype(jnp.bfloat16)
            slopes = jnp.dot(
                rowtab[...],
                jnp.concatenate([upper, lower], axis=0),
                preferred_element_type=jnp.float32,
            )
            for half in range(2):
                columns = slice(half * lanes, (half + 1) * lanes)
                high[component, first + half] = upper[:, columns]
                low[component, first + half] = lower[:, columns]
                dy[component, first + half] = slopes[:, columns] * metric[...]
        return carry

    lax.fori_loop(0, 3 * slab // 8, row_slopes, 0)

    pl.semaphore_wait(ready_sem.at[1], 2)
    greet(2)

    def lane_slopes(trip, carry):
        weights = jnp.concatenate([lanetab[...], lanetab[...]], axis=0)
        for part in range(4):
            plane = 4 * trip + part
            values = jnp.concatenate(
                [
                    high[:, plane].reshape(3 * rows, lanes),
                    low[:, plane].reshape(3 * rows, lanes),
                ],
                axis=1,
            )
            slopes = jnp.dot(values, weights, preferred_element_type=jnp.float32)
            dx[:, plane] = slopes.reshape(3, rows, lanes)
        return carry

    lax.fori_loop(0, slab // 4, lane_slopes, 0)

    pl.semaphore_wait(ready_sem.at[2], 2)
    greet(3)

    def without_lanes(plane, window):
        along = []
        for component in range(3):
            field = [vel[component, plane + k, window, :] for k in (0, 1, 2, 4, 5, 6)]
            along.append(
                45.0 * (field[3] - field[2]) - 9.0 * (field[4] - field[1]) + (field[5] - field[0])
            )
        normal = [dy[component, plane, window, :] for component in (1, 2)]
        twist = normal[1] - along[1]
        partial = normal[0] * normal[0] + along[2] * along[2] + 2.0 * (along[1] * normal[1])
        return partial, twist * twist, along[0]

    def inner_planes(part, carry):
        window = pl.ds(pl.multiple_of(part * 8, 8), 8)
        for plane in range(3, slab - 3):
            rest[plane, window, :], spin[plane, window, :], span[plane, window, :] = without_lanes(
                plane, window
            )
        return carry

    lax.fori_loop(0, rows // 8, inner_planes, 0)

    @pl.when(odd == 0)
    def _():
        pl.semaphore_wait(tile_sem, 2)
        for component in range(3):
            for rightward in (True, False):
                edge_copy(component, rightward).start()

    for component in range(3):
        for rightward in (True, False):
            edge_copy(component, rightward).wait_recv()

    wide_lane = lax.broadcasted_iota(jnp.int32, (3, rows, lanes), 2)
    halo = jnp.where(lax.rem(wide_lane, 8) < 3, from_left[...], from_right[...])
    halo_high = halo.astype(jnp.bfloat16)
    halo_low = (halo - halo_high.astype(jnp.float32)).astype(jnp.bfloat16)
    edge_parts[:, :lanes] = halo_high.reshape(3 * rows, lanes)
    edge_parts[:, lanes:] = halo_low.reshape(3 * rows, lanes)

    def edge_slopes(trip, carry):
        for part in range(2):
            pair = 2 * trip + part
            weights = jnp.concatenate([halotab[pair], halotab[pair]], axis=0)
            slopes = jnp.dot(edge_parts[...], weights, preferred_element_type=jnp.float32)
            for half in range(2):
                columns = slice(half * lanes, (half + 1) * lanes)
                dx[:, 2 * pair + half] += slopes[:, columns].reshape(3, rows, lanes)
        return carry

    lax.fori_loop(0, slab // 4, edge_slopes, 0)

    first_cell = me * slab

    def render(window):
        left_over = counts[window, :] - first_cell
        clear = jnp.ones((8, lanes), jnp.float32)
        total = jnp.zeros((8, lanes), jnp.float32)
        colour = [jnp.zeros((8, lanes), jnp.float32) for _ in range(3)]
        for plane in range(slab):
            if 3 <= plane < slab - 3:
                partial, square, along = (part[plane, window, :] for part in (rest, spin, span))
            else:
                partial, square, along = without_lanes(plane, window)
            stream = [dx[component, plane, window, :] for component in range(3)]
            normal = dy[0, plane, window, :]
            contraction = (
                partial
                + stream[0] * stream[0]
                + 2.0 * (normal * stream[1] + along * stream[2])
            )
            second, third = along - stream[2], stream[1] - normal
            square = square + second * second + third * third
            swirl = jnp.tanh(
                square * lax.rsqrt(jnp.maximum(square, 1e-30)) * (1.0 / (60.0 * VORTEX_SCALE))
            )
            scale = 0.5 * (lanes - 1)
            level = scale + scale * jnp.tanh(contraction * (-1.0 / (4.0 * 3600.0)))
            floor = jnp.minimum(jnp.floor(level), lanes - 2.0)
            fraction = level - floor
            bins = floor.astype(jnp.int32)
            values = [
                lookup(table[channel], bins) + fraction * lookup(table[4 + channel], bins)
                for channel in range(4)
            ]
            extinct = jnp.where(
                left_over > plane, values[0] * (OPTICAL_DEPTH / (slab * depth_count)), 0.0
            )
            opacity = extinct * (
                1.0 - extinct * (0.5 - extinct * (1.0 / 6.0 - extinct * (1.0 / 24.0)))
            )
            weight = clear * opacity
            clear = clear - weight
            total = total + extinct
            weight = weight * swirl
            colour = [colour[k] + weight * values[1 + k] for k in range(3)]
        return colour + [total]

    def piece_copy(owner):
        return pltpu.make_async_remote_copy(
            src_ref=pieces.at[owner],
            dst_ref=landed.at[me],
            send_sem=piece_send.at[owner],
            recv_sem=piece_recv.at[me],
            device_id={"depth": owner},
            device_id_type=MESH,
        )

    def render_chunk(step, carry):
        for upward in (True, False):
            halo_arrival(step, upward).wait()
        chunk = chunk_of(me, step)

        def render_rows(part, carry):
            window = pl.ds(pl.multiple_of(chunk * chunk_rows + part * 8, 8), 8)
            for channel, image in enumerate(render(window)):
                stage[channel, pl.ds(pl.multiple_of(part * 8, 8), 8), :] = image
            return carry

        lax.fori_loop(0, chunk_rows // 8, render_rows, 0)
        for row in range(3):
            for channel in range(4):
                spread = stage.at[channel][pl.ds(row, owners, stride=3), :]
                for owner in range(owners):
                    pieces[chunk * owners + owner, row, pl.ds(channel, 1), :] = spread[
                        owner : owner + 1
                    ]

        @pl.when(step == 0)
        def _():
            pl.semaphore_wait(ready_sem.at[3], 2)

        def send(place, carry):
            owner = chunk * owners + place

            @pl.when(owner != me)
            def _():
                piece_copy(owner).start()

            return carry

        lax.fori_loop(0, owners, send, 0)
        return carry

    lax.fori_loop(0, CHUNKS, render_chunk, 0)
    landed[me] = pieces[me]

    def receive(place, carry):
        @pl.when(place != me)
        def _():
            pltpu.make_async_copy(landed.at[place], landed.at[place], piece_recv.at[place]).wait()

        return carry

    lax.fori_loop(0, depth_count, receive, 0)

    before = jnp.zeros((3, 4, lanes), jnp.float32)
    image = jnp.zeros((3, 4, lanes), jnp.float32)
    for device in range(depth_count):
        part = landed[device]
        image = image + jnp.exp(-before) * part
        before = before + jnp.broadcast_to(landed[device, :, 3:4, :], (3, 4, lanes))
    channels = lax.broadcasted_iota(jnp.int32, (3, 4, lanes), 1)
    out_ref[...] = jnp.where(channels == 3, before, image)

    def sent(place, carry):
        @pl.when(place != me)
        def _():
            piece_copy(place).wait_send()

        return carry

    lax.fori_loop(0, depth_count, sent, 0)
    for component in range(3):
        for rightward in (True, False):
            edge_copy(component, rightward).wait_send()
    for step in range(CHUNKS):
        for upward in (True, False):
            halo_copy(step, upward).wait_send()


def per_device(depth_count, tile_count, velocity, metric, colour_map, counts):
    slab, rows, lanes = velocity.shape[1:]
    tables = stencil_tables(slab, rows, lanes)
    f32, bf16 = jnp.float32, jnp.bfloat16
    operands = (
        velocity,
        metric.reshape(1, rows),
        colour_map,
        counts,
        *(jnp.asarray(table) for table in tables),
    )
    block = (slab, rows, lanes)
    result = pl.pallas_call(
        functools.partial(kernel, depth_count, tile_count),
        out_shape=jax.ShapeDtypeStruct((rows // depth_count, 4, lanes), f32),
        in_specs=[pl.BlockSpec(memory_space=pl.ANY)] * len(operands),
        out_specs=pl.BlockSpec(memory_space=pltpu.VMEM),
        scratch_shapes=[
            pltpu.VMEM((3, slab + 6, rows, lanes), f32),
            pltpu.VMEM((3, *block), bf16),
            pltpu.VMEM((3, *block), bf16),
            pltpu.VMEM((3, *block), f32),
            pltpu.VMEM((3, *block), f32),
            pltpu.VMEM(block, f32),
            pltpu.VMEM(block, f32),
            pltpu.VMEM(block, f32),
            pltpu.VMEM((1, rows), f32),
            pltpu.VMEM((rows, lanes), f32),
            pltpu.VMEM(colour_map.shape, bf16),
            pltpu.VMEM((8, 8, lanes), f32),
            pltpu.VMEM((rows, lanes), jnp.int32),
            *(pltpu.VMEM(table.shape, bf16) for table in tables),
            pltpu.VMEM((3, rows, lanes), f32),
            pltpu.VMEM((3, rows, lanes), f32),
            pltpu.VMEM((3, rows, lanes), f32),
            pltpu.VMEM((3 * rows, 2 * lanes), bf16),
            pltpu.VMEM((4, rows // CHUNKS, lanes), f32),
            pltpu.VMEM((depth_count, rows // depth_count, 4, lanes), f32),
            pltpu.VMEM((depth_count, rows // depth_count, 4, lanes), f32),
            pltpu.SemaphoreType.DMA((9,)),
            pltpu.SemaphoreType.DMA((2, 3)),
            pltpu.SemaphoreType.DMA((2, 3)),
            pltpu.SemaphoreType.DMA((2, CHUNKS)),
            pltpu.SemaphoreType.DMA((2, CHUNKS)),
            pltpu.SemaphoreType.DMA((depth_count,)),
            pltpu.SemaphoreType.DMA((depth_count,)),
            pltpu.SemaphoreType.REGULAR((4,)),
            pltpu.SemaphoreType.REGULAR,
        ],
        compiler_params=pltpu.CompilerParams(
            collective_id=0, has_side_effects=True, vmem_limit_bytes=60 * 1024 * 1024
        ),
    )(*operands)
    channel = lax.broadcasted_iota(jnp.int32, result.shape, 1)
    return jnp.where(channel == 3, -jnp.expm1(-result), result).transpose(1, 0, 2)


def solution(mesh):
    in_specs = (P(None, "depth", None, "tile"), P(), P(), P(None, "tile"))
    out_specs = P(None, "depth", "tile")
    return jax.shard_map(
        functools.partial(per_device, mesh.shape["depth"], mesh.shape["tile"]),
        mesh=mesh,
        in_specs=in_specs,
        out_specs=out_specs,
        check_vma=False,
    )
```

time: 36.9 us -> 32.2 us (0.87)
  the two profiles are of different devices: /device:TPU:6 before, /device:TPU:193 now
where the time goes in v2:
time: 32.2 us; the launch traced here: 32 us
  Pallas kernels  30.7 us (95%)
  other arithmetic  1.36 us (4%)
    pallas_call x1, Pallas kernels, per_device(): pl.pallas_call(functools.partial(kernel, depth_count, tile_count), out_sh...  30.7 us
    transpose x1, other arithmetic, per_device(): jnp.where(channel == 3, -jnp.expm1(-result), result).transpose(1, 0, 2)  1.36 us

profile of v2, /device:TPU:193, one launch (start us, length us, event | category | flops | bytes accessed | tf_op | source)
XLA Modules:
  0.0 32.0 jit_solution(1044065304407841885)
XLA Ops:
  0.0 30.7 %shard_map.73 = f32[3,4,128]{2,1,0:T(4,128)} custom-call(f32[3,16,96,128]{3,2,1,0:T(8,128)} %vel_hbm.1, f32[1,96]{1,0:T(1,128)} %bitcast.3, bf16[4,128]{1,0:T(4,128)(2,1)} %map_hbm.1, s32[96,128]{1,0:T(8,128)} %counts_hbm.1, bf16[96,192]{1,0:T(8,128)(2,1)} %constant.8.clone.rowtab_hbm, bf16[128,128]{1,0:T(8,128)(2,1)} %constant.9.clone.lanetab_hbm, ...), custom_call_target="tpu_custom_call" | custom-call | tf_op jit(solution)/shard_map/pallas_call | solution.py:476
  30.7 1.4 %select_bitcast_fusion = f32[4,3,128]{2,0,1:T(4,128)} fusion(f32[3,4,128]{2,1,0:T(4,128)} %shard_map.73, pred[4]{0:T(512)(128)(4,1)S(1)} %iota_compare_fusion), kind=kLoop, calls=%fused_computation | loop fusion | flops 4608 | bytes 12292 | tf_op jit(solution)/shard_map/transpose | solution.py:518
  (1 shorter events, 0.0 us)

commit v3 on v2

--- a/solution.py
+++ b/solution.py
@@ -12,6 +12,7 @@
 VORTEX_SCALE = 4.0
 OPTICAL_DEPTH = 4.0
 CHUNKS = 4
+TABLE_SCALE = 16384.0
 MESH = pl.DeviceIdType.MESH
 ALONG_LANES = lax.GatherDimensionNumbers(
     offset_dims=(),
@@ -108,8 +109,18 @@
     right, left = lax.rem(tile + 1, tile_count), lax.rem(tile + tile_count - 1, tile_count)
 
     barrier = pltpu.get_barrier_semaphore()
-    for peer in (up, down):
-        pl.semaphore_signal(barrier, inc=1, device_id={"depth": peer}, device_id_type=MESH)
+
+    def greet(semaphore, peers):
+        for peer in peers:
+            pl.semaphore_signal(semaphore, inc=1, device_id={"depth": peer}, device_id_type=MESH)
+
+    def greet_level(level):
+        greet(
+            ready_sem.at[level],
+            [lax.rem(me + shift, depth_count) for shift in (2**level, depth_count - 2**level)],
+        )
+
+    greet(barrier, [up, down])
 
     @pl.when(odd == 0)
     def _():
@@ -141,27 +152,29 @@
             CHUNKS,
         )
 
-    def chunk_at(device, step):
-        return pl.ds(pl.multiple_of(chunk_of(device, step) * chunk_rows, 8), chunk_rows)
-
-    def halo_copy(step, upward):
+    tiles = chunk_rows // 8
+
+    def rows_at(device, place):
+        first = chunk_of(device, place // tiles) * chunk_rows + lax.rem(place, tiles) * 8
+        return pl.ds(pl.multiple_of(first, 8), 8)
+
+    def halo_copy(place, upward):
         target = up if upward else down
-        window = chunk_at(target, step)
-        first, place = (slab - 3, 0) if upward else (0, slab + 3)
+        window = rows_at(target, place)
+        source, landing = (slab - 3, 0) if upward else (0, slab + 3)
         return pltpu.make_async_remote_copy(
-            src_ref=vel_hbm.at[:, pl.ds(first, 3), window, :],
-            dst_ref=vel.at[:, pl.ds(place, 3), window, :],
-            send_sem=halo_send.at[int(upward), step],
-            recv_sem=halo_recv.at[int(upward), step],
+            src_ref=vel_hbm.at[:, pl.ds(source, 3), window, :],
+            dst_ref=vel.at[:, pl.ds(landing, 3), window, :],
+            send_sem=halo_send.at[int(upward), place],
+            recv_sem=halo_recv.at[int(upward), place],
             device_id={"depth": target},
             device_id_type=MESH,
         )
 
-    def halo_arrival(step, upward):
-        window = chunk_at(me, step)
-        place = 0 if upward else slab + 3
-        part = vel.at[:, pl.ds(place, 3), window, :]
-        return pltpu.make_async_copy(part, part, halo_recv.at[int(upward), step])
+    def halo_arrival(place, upward):
+        landing = 0 if upward else slab + 3
+        part = vel.at[:, pl.ds(landing, 3), rows_at(me, place), :]
+        return pltpu.make_async_copy(part, part, halo_recv.at[int(upward), place])
 
     def edge_copy(component, rightward):
         target = (from_left if rightward else from_right).at[component]
@@ -174,20 +187,15 @@
             device_id_type=MESH,
         )
 
-    def greet(level):
-        for peer in (
-            lax.rem(me + 2**level, depth_count),
-            lax.rem(me + depth_count - 2**level, depth_count),
-        ):
-            pl.semaphore_signal(
-                ready_sem.at[level], inc=1, device_id={"depth": peer}, device_id_type=MESH
-            )
-
     pl.semaphore_wait(barrier, 2 + 2 * odd)
-    for step in range(CHUNKS):
+
+    def send_halo(place, carry):
         for upward in (True, False):
-            halo_copy(step, upward).start()
-    greet(0)
+            halo_copy(place, upward).start()
+        return carry
+
+    lax.fori_loop(0, rows // 8, send_halo, 0)
+    greet_level(0)
 
     @pl.when(odd == 1)
     def _():
@@ -216,8 +224,15 @@
             for rightward in (True, False):
                 edge_copy(component, rightward).start()
 
+    def answer():
+        pl.semaphore_wait(tile_sem, 2)
+        for component in range(3):
+            for rightward in (True, False):
+                edge_copy(component, rightward).start()
+
+    pl.when((odd == 0) & (tile != 0))(answer)
     pl.semaphore_wait(ready_sem.at[0], 2)
-    greet(1)
+    greet_level(1)
 
     for load in loads[3:]:
         load.wait()
@@ -230,11 +245,11 @@
         keepdims=True,
     )
     metric[...] = jnp.broadcast_to(column, (rows, lanes))
-    entries = map_in[...].astype(jnp.float32)
-    steps = pltpu.roll(entries, lanes - 1, 1) - entries
+    entries = map_in[...].astype(jnp.float32) * TABLE_SCALE
+    following = pltpu.roll(entries, lanes - 1, 1).astype(jnp.int32)
+    both = entries.astype(jnp.int32) * 65536 + following
     for channel in range(4):
-        table[channel] = jnp.broadcast_to(entries[channel : channel + 1], (8, lanes))
-        table[4 + channel] = jnp.broadcast_to(steps[channel : channel + 1], (8, lanes))
+        table[channel] = jnp.broadcast_to(both[channel : channel + 1], (8, lanes))
 
     def row_slopes(trip, carry):
         component = trip // 2
@@ -258,7 +273,8 @@
     lax.fori_loop(0, 3 * slab // 8, row_slopes, 0)
 
     pl.semaphore_wait(ready_sem.at[1], 2)
-    greet(2)
+    greet_level(2)
+    pl.when(tile == 0)(answer)
 
     def lane_slopes(trip, carry):
         weights = jnp.concatenate([lanetab[...], lanetab[...]], axis=0)
@@ -278,7 +294,7 @@
     lax.fori_loop(0, slab // 4, lane_slopes, 0)
 
     pl.semaphore_wait(ready_sem.at[2], 2)
-    greet(3)
+    greet_level(3)
 
     def without_lanes(plane, window):
         along = []
@@ -301,13 +317,6 @@
         return carry
 
     lax.fori_loop(0, rows // 8, inner_planes, 0)
-
-    @pl.when(odd == 0)
-    def _():
-        pl.semaphore_wait(tile_sem, 2)
-        for component in range(3):
-            for rightward in (True, False):
-                edge_copy(component, rightward).start()
 
     for component in range(3):
         for rightward in (True, False):
@@ -361,12 +370,15 @@
             floor = jnp.minimum(jnp.floor(level), lanes - 2.0)
             fraction = level - floor
             bins = floor.astype(jnp.int32)
-            values = [
-                lookup(table[channel], bins) + fraction * lookup(table[4 + channel], bins)
-                for channel in range(4)
-            ]
+            remainder = 1.0 - fraction
+            values = []
+            for channel in range(4):
+                pair = lookup(table[channel], bins)
+                lower = lax.shift_right_logical(pair, 16).astype(jnp.float32)
+                upper = (pair & 65535).astype(jnp.float32)
+                values.append(remainder * lower + fraction * upper)
             extinct = jnp.where(
-                left_over > plane, values[0] * (OPTICAL_DEPTH / (slab * depth_count)), 0.0
+                left_over > plane, values[0] * (OPTICAL_DEPTH / (slab * depth_count * TABLE_SCALE)), 0.0
             )
             opacity = extinct * (
                 1.0 - extinct * (0.5 - extinct * (1.0 / 6.0 - extinct * (1.0 / 24.0)))
@@ -376,24 +388,24 @@
             total = total + extinct
             weight = weight * swirl
             colour = [colour[k] + weight * values[1 + k] for k in range(3)]
-        return colour + [total]
+        return [part * (1.0 / TABLE_SCALE) for part in colour] + [total]
 
     def piece_copy(owner):
         return pltpu.make_async_remote_copy(
             src_ref=pieces.at[owner],
             dst_ref=landed.at[me],
-            send_sem=piece_send.at[owner],
-            recv_sem=piece_recv.at[me],
+            send_sem=piece_send,
+            recv_sem=piece_recv,
             device_id={"depth": owner},
             device_id_type=MESH,
         )
 
     def render_chunk(step, carry):
-        for upward in (True, False):
-            halo_arrival(step, upward).wait()
         chunk = chunk_of(me, step)
 
         def render_rows(part, carry):
+            for upward in (True, False):
+                halo_arrival(step * tiles + part, upward).wait()
             window = pl.ds(pl.multiple_of(chunk * chunk_rows + part * 8, 8), 8)
             for channel, image in enumerate(render(window)):
                 stage[channel, pl.ds(pl.multiple_of(part * 8, 8), 8), :] = image
@@ -427,14 +439,8 @@
     lax.fori_loop(0, CHUNKS, render_chunk, 0)
     landed[me] = pieces[me]
 
-    def receive(place, carry):
-        @pl.when(place != me)
-        def _():
-            pltpu.make_async_copy(landed.at[place], landed.at[place], piece_recv.at[place]).wait()
-
-        return carry
-
-    lax.fori_loop(0, depth_count, receive, 0)
+    others = landed.at[pl.ds(0, depth_count - 1)]
+    pltpu.make_async_copy(others, others, piece_recv).wait()
 
     before = jnp.zeros((3, 4, lanes), jnp.float32)
     image = jnp.zeros((3, 4, lanes), jnp.float32)
@@ -445,20 +451,17 @@
     channels = lax.broadcasted_iota(jnp.int32, (3, 4, lanes), 1)
     out_ref[...] = jnp.where(channels == 3, before, image)
 
-    def sent(place, carry):
-        @pl.when(place != me)
-        def _():
-            piece_copy(place).wait_send()
-
-        return carry
-
-    lax.fori_loop(0, depth_count, sent, 0)
+    pltpu.make_async_copy(others, others, piece_send).wait()
     for component in range(3):
         for rightward in (True, False):
             edge_copy(component, rightward).wait_send()
-    for step in range(CHUNKS):
+
+    def halo_sent(place, carry):
         for upward in (True, False):
-            halo_copy(step, upward).wait_send()
+            halo_copy(place, upward).wait_send()
+        return carry
+
+    lax.fori_loop(0, rows // 8, halo_sent, 0)
 
 
 def per_device(depth_count, tile_count, velocity, metric, colour_map, counts):
@@ -490,7 +493,7 @@
             pltpu.VMEM((1, rows), f32),
             pltpu.VMEM((rows, lanes), f32),
             pltpu.VMEM(colour_map.shape, bf16),
-            pltpu.VMEM((8, 8, lanes), f32),
+            pltpu.VMEM((4, 8, lanes), jnp.int32),
             pltpu.VMEM((rows, lanes), jnp.int32),
             *(pltpu.VMEM(table.shape, bf16) for table in tables),
             pltpu.VMEM((3, rows, lanes), f32),
@@ -503,10 +506,10 @@
             pltpu.SemaphoreType.DMA((9,)),
             pltpu.SemaphoreType.DMA((2, 3)),
             pltpu.SemaphoreType.DMA((2, 3)),
-            pltpu.SemaphoreType.DMA((2, CHUNKS)),
-            pltpu.SemaphoreType.DMA((2, CHUNKS)),
-            pltpu.SemaphoreType.DMA((depth_count,)),
-            pltpu.SemaphoreType.DMA((depth_count,)),
+            pltpu.SemaphoreType.DMA((2, rows // 8)),
+            pltpu.SemaphoreType.DMA((2, rows // 8)),
+            pltpu.SemaphoreType.DMA,
+            pltpu.SemaphoreType.DMA,
             pltpu.SemaphoreType.REGULAR((4,)),
             pltpu.SemaphoreType.REGULAR,
         ],

time: 32.2 us -> 28.6 us (0.89)
  the two profiles are of different devices: /device:TPU:193 before, /device:TPU:22 now
where the time goes in v3:
time: 28.6 us; the launch traced here: 28.4 us
  Pallas kernels  27.1 us (95%)
  other arithmetic  1.36 us (5%)
    pallas_call x1, Pallas kernels, per_device(): pl.pallas_call(functools.partial(kernel, depth_count, tile_count), out_sh...  27.1 us
    transpose x1, other arithmetic, per_device(): jnp.where(channel == 3, -jnp.expm1(-result), result).transpose(1, 0, 2)  1.36 us

profile of v3, /device:TPU:22, one launch (start us, length us, event | category | flops | bytes accessed | tf_op | source)
XLA Modules:
  0.0 28.4 jit_solution(275011528313070193)
XLA Ops:
  0.0 27.1 %shard_map.73 = f32[3,4,128]{2,1,0:T(4,128)} custom-call(f32[3,16,96,128]{3,2,1,0:T(8,128)} %vel_hbm.1, f32[1,96]{1,0:T(1,128)} %bitcast.3, bf16[4,128]{1,0:T(4,128)(2,1)} %map_hbm.1, s32[96,128]{1,0:T(8,128)} %counts_hbm.1, bf16[96,192]{1,0:T(8,128)(2,1)} %constant.8.clone.rowtab_hbm, bf16[128,128]{1,0:T(8,128)(2,1)} %constant.9.clone.lanetab_hbm, ...), custom_call_target="tpu_custom_call" | custom-call | tf_op jit(solution)/shard_map/pallas_call | solution.py:479
  27.1 1.4 %select_bitcast_fusion = f32[4,3,128]{2,0,1:T(4,128)} fusion(f32[3,4,128]{2,1,0:T(4,128)} %shard_map.73, pred[4]{0:T(512)(128)(4,1)S(1)} %iota_compare_fusion), kind=kLoop, calls=%fused_computation | loop fusion | flops 4608 | bytes 12292 | tf_op jit(solution)/shard_map/transpose | solution.py:521
  (1 shorter events, 0.0 us)

commit v4 on v3

--- a/solution.py
+++ b/solution.py
@@ -82,6 +82,7 @@
     lanetab,
     halotab,
     edge,
+    outgoing,
     from_left,
     from_right,
     edge_parts,
@@ -179,7 +180,7 @@
     def edge_copy(component, rightward):
         target = (from_left if rightward else from_right).at[component]
         return pltpu.make_async_remote_copy(
-            src_ref=edge.at[component],
+            src_ref=outgoing.at[int(rightward), component],
             dst_ref=target,
             send_sem=edge_send.at[int(rightward), component],
             recv_sem=edge_recv.at[int(rightward), component],
@@ -218,6 +219,12 @@
             return carry
 
         lax.fori_loop(0, rows // 24, pack, 0)
+        first, second = edge[component, : rows // 2], edge[component, rows // 2 :]
+        slot = lax.rem(lax.broadcasted_iota(jnp.int32, first.shape, 1), 8)
+        outgoing[1, component] = jnp.where(slot < 4, first, pltpu.roll(second, 4, 1))
+        outgoing[0, component] = jnp.where(
+            slot < 4, pltpu.roll(first, lanes - 3, 1), pltpu.roll(second, 1, 1)
+        )
 
         @pl.when(odd == 1)
         def _():
@@ -322,12 +329,18 @@
         for rightward in (True, False):
             edge_copy(component, rightward).wait_recv()
 
-    wide_lane = lax.broadcasted_iota(jnp.int32, (3, rows, lanes), 2)
-    halo = jnp.where(lax.rem(wide_lane, 8) < 3, from_left[...], from_right[...])
-    halo_high = halo.astype(jnp.bfloat16)
-    halo_low = (halo - halo_high.astype(jnp.float32)).astype(jnp.bfloat16)
-    edge_parts[:, :lanes] = halo_high.reshape(3 * rows, lanes)
-    edge_parts[:, lanes:] = halo_low.reshape(3 * rows, lanes)
+    for component in range(3):
+        before, after = from_left[component], from_right[component]
+        slot = lax.rem(lax.broadcasted_iota(jnp.int32, before.shape, 1), 8)
+        upper_rows = jnp.where(slot < 3, before, pltpu.roll(after, 3, 1))
+        lower_rows = jnp.where(
+            slot < 3, pltpu.roll(before, lanes - 4, 1), pltpu.roll(after, lanes - 1, 1)
+        )
+        halo = jnp.concatenate([upper_rows, lower_rows], axis=0)
+        halo_high = halo.astype(jnp.bfloat16)
+        window = pl.ds(component * rows, rows)
+        edge_parts[window, :lanes] = halo_high
+        edge_parts[window, lanes:] = (halo - halo_high.astype(jnp.float32)).astype(jnp.bfloat16)
 
     def edge_slopes(trip, carry):
         for part in range(2):
@@ -497,8 +510,9 @@
             pltpu.VMEM((rows, lanes), jnp.int32),
             *(pltpu.VMEM(table.shape, bf16) for table in tables),
             pltpu.VMEM((3, rows, lanes), f32),
-            pltpu.VMEM((3, rows, lanes), f32),
-            pltpu.VMEM((3, rows, lanes), f32),
+            pltpu.VMEM((2, 3, rows // 2, lanes), f32),
+            pltpu.VMEM((3, rows // 2, lanes), f32),
+            pltpu.VMEM((3, rows // 2, lanes), f32),
             pltpu.VMEM((3 * rows, 2 * lanes), bf16),
             pltpu.VMEM((4, rows // CHUNKS, lanes), f32),
             pltpu.VMEM((depth_count, rows // depth_count, 4, lanes), f32),

time: 28.6 us -> 28.6 us (level)
  no operation moved by 1% of the time
where the time goes in v4:
time: 28.6 us; the launch traced here: 28.4 us
  Pallas kernels  27 us (94%)
  other arithmetic  1.36 us (5%)
    pallas_call x1, Pallas kernels, per_device(): pl.pallas_call(functools.partial(kernel, depth_count, tile_count), out_sh...  27 us
    transpose x1, other arithmetic, per_device(): jnp.where(channel == 3, -jnp.expm1(-result), result).transpose(1, 0, 2)  1.36 us

profile of v4, /device:TPU:22, one launch (start us, length us, event | category | flops | bytes accessed | tf_op | source)
XLA Modules:
  0.0 28.4 jit_solution(11705829344219055885)
XLA Ops:
  0.0 27.0 %shard_map.73 = f32[3,4,128]{2,1,0:T(4,128)} custom-call(f32[3,16,96,128]{3,2,1,0:T(8,128)} %vel_hbm.1, f32[1,96]{1,0:T(1,128)} %bitcast.3, bf16[4,128]{1,0:T(4,128)(2,1)} %map_hbm.1, s32[96,128]{1,0:T(8,128)} %counts_hbm.1, bf16[96,192]{1,0:T(8,128)(2,1)} %constant.8.clone.rowtab_hbm, bf16[128,128]{1,0:T(8,128)(2,1)} %constant.9.clone.lanetab_hbm, ...), custom_call_target="tpu_custom_call" | custom-call | tf_op jit(solution)/shard_map/pallas_call | solution.py:492
  27.1 1.4 %select_bitcast_fusion = f32[4,3,128]{2,0,1:T(4,128)} fusion(f32[3,4,128]{2,1,0:T(4,128)} %shard_map.73, pred[4]{0:T(512)(128)(4,1)S(1)} %iota_compare_fusion), kind=kLoop, calls=%fused_computation | loop fusion | flops 4608 | bytes 12292 | tf_op jit(solution)/shard_map/transpose | solution.py:535
  (1 shorter events, 0.0 us)
